TPU v7x, 32 devices: a whole 2x2x4 slice. The times are simulated.
32 devices in a mesh: parts: 2 (over y), step: 4 (over z), frame: 2 (over x), head: 2 (over core).
Axes of the slice: x: 2, y: 2, z: 4, core: 2. Of those that a mesh axis runs over, the one named last changes fastest.
Arguments:
- start_noise: float32 [32, 256], P('parts', 'frame'), parts along dimension 0, may hold values from -6 to 6
- position: bfloat16 [256, 1152], P('frame'), may hold values from -6 to 6
- time_table: bfloat16 [128, 1152], replicated, may hold values from -6 to 6
- time_index: int32 [4], P('step'), may hold values from 0 to 127
- sched_index: int32 [4], P('step'), may hold values from 0 to 127
- coef_keep: float32 [128], replicated, may hold values from -0.06 to -0.01
- coef_noise: float32 [128], replicated, may hold values from 0.03 to 0.12
- w_in: bfloat16 [16, 1152], replicated, may hold values from -1.5 to 1.5
- norm_gain: float32 [1152], replicated, may hold values from 0.5 to 1.5
- w_qkv: bfloat16 [1152, 3, 1152], P('step', None, 'head'), may hold values from -4 to 4
- w_proj: bfloat16 [1152, 1152], P('step', 'head'), may hold values from -0.1875 to 0.1875
- w_final: bfloat16 [16, 1152], replicated, may hold values from -0.1875 to 0.1875
Outputs:
- trajectory: float32 [4, 32, 256], P('step', 'parts', 'frame'), parts along dimension 1
- residual_norms: float32 [8], P('parts'), parts along dimension 0
There are 2 independent parts, one for each index of `parts`. A program takes and returns all parts, laid end to end along the dimension named above; an argument that names none is the same for every part. Nothing has to cross between parts.
All inputs are finite; a program needn't handle non-finite values.
Results may differ from a plain program's by a relative error of at most 0.0044.
Values may be sent and summed in bfloat16 or wider, within the bound.
A program may use at most 64 MiB of HBM per device.

v0:
```python
import math

import jax
import jax.numpy as jnp
from jax import lax
from jax.sharding import PartitionSpec as P

HDIM = 72
ITERS = 4


def entering(value, axis, combine, identity):
    count, here = (lax.axis_size(axis), lax.axis_index(axis))
    everything = lax.all_gather(value, axis)
    start = jnp.broadcast_to(jnp.asarray(identity, value.dtype), value.shape)

    def hop(k, before):
        reached = k < here
        new = combine(before, everything[k])
        return jnp.where(reached, new, before)

    return lax.fori_loop(0, count, hop, start)


def add_terms(first, second):
    return first + second


def local(
    start_noise,
    position,
    time_table,
    time_index,
    sched_index,
    coef_keep,
    coef_noise,
    w_in,
    norm_gain,
    w_qkv,
    w_proj,
    w_final,
):
    w_qkv_all, w_proj_all = (
        lax.all_gather(w_qkv, "step", axis=0, tiled=True),
        lax.all_gather(w_proj, "step", axis=0, tiled=True),
    )
    batch_steps = time_index.shape[0]
    row_count = start_noise.shape[1]
    table_rows = time_table.shape[0]
    pick_time = (time_index[:, None] == jnp.arange(table_rows)[None, :]).astype(jnp.bfloat16)
    time_embed = jnp.dot(pick_time, time_table, preferred_element_type=jnp.float32)
    pick_sched = (sched_index[:, None] == jnp.arange(table_rows)[None, :]).astype(jnp.float32)
    keep_rate = jnp.sum(pick_sched * coef_keep[None, :], axis=1)
    noise_rate = jnp.sum(pick_sched * coef_noise[None, :], axis=1)
    heads_local = w_qkv_all.shape[2] // HDIM
    cell_count = (
        batch_steps
        * lax.axis_size("step")
        * start_noise.shape[0]
        * row_count
        * lax.axis_size("frame")
    )
    states = start_noise[None]
    drift_term = jnp.zeros_like(states)
    residual_list = []
    for iteration in range(ITERS):
        latent_bf = states.astype(jnp.bfloat16)
        hidden = (
            jnp.einsum("bcr,cd->brd", latent_bf, w_in, preferred_element_type=jnp.float32)
            + position
            + time_embed[:, None, :]
        )
        normed = (
            hidden * lax.rsqrt(jnp.mean(hidden * hidden, axis=2, keepdims=True) + 1e-06) * norm_gain
        ).astype(jnp.bfloat16)
        projected = jnp.einsum(
            "brd,dkq->brkq", normed, w_qkv_all, preferred_element_type=jnp.float32
        ).astype(jnp.bfloat16)
        queries = projected[:, :, 0].reshape(batch_steps, row_count, heads_local, HDIM)
        score_scale = 1.0 / math.sqrt(HDIM)
        keys_values = projected[:, :, 1:3]
        piece = lax.all_gather(keys_values, "frame", axis=1, tiled=True)
        top_old = jnp.full((batch_steps, heads_local, row_count), -1e30, jnp.float32)
        piece_rows = piece.shape[1]
        keys_blk = piece[:, :, 0].reshape(batch_steps, piece_rows, heads_local, HDIM)
        values_blk = piece[:, :, 1].reshape(batch_steps, piece_rows, heads_local, HDIM)
        scores = (
            jnp.einsum("bqhe,bkhe->bhqk", queries, keys_blk, preferred_element_type=jnp.float32)
            * score_scale
        )
        top_new = jnp.maximum(top_old, jnp.max(scores, axis=3))
        weights_exp = jnp.exp(scores - top_new[:, :, :, None])
        total_new = jnp.sum(weights_exp, axis=3)
        update = jnp.einsum(
            "bhqk,bkhe->bqhe",
            weights_exp.astype(jnp.bfloat16),
            values_blk,
            preferred_element_type=jnp.float32,
        )
        accum = update
        top_final, total_final, accum = (top_new, total_new, accum)
        attended = accum / jnp.transpose(total_final, (0, 2, 1))[:, :, :, None]
        attn_mixed = attended.reshape(batch_steps, row_count, heads_local * HDIM).astype(
            jnp.bfloat16
        )
        partial_value = jnp.einsum(
            "brq,dq->brd", attn_mixed, w_proj_all, preferred_element_type=jnp.float32
        )
        head_total = lax.psum(partial_value, "head")
        joined = (hidden + head_total).astype(jnp.bfloat16)
        predicted = jnp.einsum("cd,brd->bcr", w_final, joined, preferred_element_type=jnp.float32)
        drift_term = keep_rate[:, None, None] * states + noise_rate[:, None, None] * predicted
        local_incl = jnp.cumsum(drift_term, axis=0)
        local_total = local_incl[-1]
        earlier = entering(local_total, "step", add_terms, jnp.zeros_like(local_total))
        before = earlier[None] + (local_incl - drift_term)
        new_states = start_noise[None] + before
        change = new_states - states
        square_sum = jnp.sum(change * change)
        summed = lax.psum(square_sum, ("step", "frame"))
        residual_list.append(jnp.sqrt(summed / cell_count + 1e-06))
        states = new_states
    residual_norms = jnp.stack(residual_list)
    trajectory = states + drift_term
    return (trajectory, residual_norms)


def solution(mesh):
    return jax.shard_map(
        local,
        mesh=mesh,
        in_specs=(
            P("parts", "frame"),
            P("frame", None),
            P(),
            P("step"),
            P("step"),
            P(),
            P(),
            P(),
            P(),
            P("step", None, "head"),
            P("step", "head"),
            P(),
        ),
        out_specs=(P("step", "parts", "frame"), P("parts")),
        check_vma=False,
    )
```

profile of v0, /device:TPU:0, one launch (start us, length us, event | category | flops | bytes accessed | tf_op | source)
XLA Modules:
  0.0 354.4 jit_solution(680078700515391486)
XLA Ops:
  7.3 0.7 all-gather.3.cloned.1.call-update
  8.0 0.7 all-gather.5.cloned.1.call-update
  10.0 86.9 %all-gather.3.cloned.1.call-done = bf16[1152,3,576]{2,0,1:T(8,128)(2,1)} async-done(((bf16[288,3,576]{2,0,1:T(8,128)(2,1)}), bf16[1152,3,576]{2,0,1:T(8,128)(2,1)}) %all-gather.3.cloned.1.call-update) | async-done | bytes 3981328 | tf_op jit(solution)/shard_map/all_gather | solution.py:44
  96.9 4.0 %fusion.4 = bf16[1,128,3,576]{1,3,2,0:T(8,128)(2,1)S(1)} fusion(bf16[1152,3,576]{2,0,1:T(8,128)(2,1)} %all-gather.3.cloned.1.call-done, f32[128,1152]{1,0:T(8,128)S(1)} %get-tuple-element.432, f32[1152]{0:T(1024)S(1)} %copy-done.6, f32[128]{0:T(128)S(1)} %add_rsqrt_fusion.3), kind=kOutput, calls=%fused_computation.24 | convolution fusion | flops 510271488 | bytes 5018624 | tf_op jit(solution)/shard_map/brd,dkq->brkq/dot_general | solution.py:76
  101.0 9.3 %all_gather.31 = bf16[1,256,2,576]{1,3,2,0:T(8,128)(2,1)S(1)} all-gather(bf16[1,128,2,576]{1,3,2,0:T(8,128)(2,1)S(1)} %slice.64), channel_id=1, replica_groups=mesh['parts'=2,'step'=4,'frame'=2,'head'=2] {'frame'}, dimensions={1}, use_global_device_ids=true | all-gather | bytes 884736 | tf_op jit(solution)/shard_map/all_gather | solution.py:82
  111.6 20.7 %all-gather.5.cloned.1.call-done = bf16[1152,576]{1,0:T(8,128)(2,1)} async-done(((bf16[288,576]{1,0:T(8,128)(2,1)}), bf16[1152,576]{1,0:T(8,128)(2,1)}) %all-gather.5.cloned.1.call-update) | async-done | bytes 1327120 | tf_op jit(solution)/shard_map/all_gather | solution.py:45
  132.3 2.8 convolution_bitcast_fusion.3
  135.8 0.6 fusion.84
  136.5 16.4 %all-reduce.6.cloned.1.call-done = f32[1,128,1152]{2,1,0:T(8,128)} async-done(((f32[1,128,1152]{2,1,0:T(8,128)}), f32[1,128,1152]{2,1,0:T(8,128)}) %all-reduce.6.cloned.1.call-update) | async-done | bytes 589840 | tf_op jit(solution)/shard_map/psum | solution.py:109
  152.9 2.5 fusion.15
  155.4 13.5 %all_gather.33 = f32[4,16,128]{2,1,0:T(8,128)S(1)} all-gather(f32[1,16,128]{2,1,0:T(8,128)S(1)} %fusion.15), channel_id=1, replica_groups=mesh['parts'=2,'step'=4,'frame'=2,'head'=2] {'step'}, dimensions={0}, use_global_device_ids=true | all-gather | bytes 40960 | tf_op jit(solution)/shard_map/all_gather | solution.py:14
  169.4 4.0 %fusion.5 = bf16[1,128,3,576]{1,3,2,0:T(8,128)(2,1)S(1)} fusion(bf16[1152,3,576]{2,0,1:T(8,128)(2,1)} %all-gather.3.cloned.1.call-done, f32[128,1152]{1,0:T(8,128)S(1)} %get-tuple-element.436, f32[128]{0:T(128)S(1)} %add_rsqrt_fusion.2, f32[1152]{0:T(1024)S(1)} %copy-done.6), kind=kOutput, calls=%fused_computation.25 | convolution fusion | flops 510271488 | bytes 5018624 | tf_op jit(solution)/shard_map/brd,dkq->brkq/dot_general | solution.py:76
  173.5 7.4 %all_gather.34 = bf16[1,256,2,576]{1,3,2,0:T(8,128)(2,1)S(1)} all-gather(bf16[1,128,2,576]{1,3,2,0:T(8,128)(2,1)S(1)} %slice.68), channel_id=1, replica_groups=mesh['parts'=2,'step'=4,'frame'=2,'head'=2] {'frame'}, dimensions={1}, use_global_device_ids=true | all-gather | bytes 884736 | tf_op jit(solution)/shard_map/all_gather | solution.py:82
  182.8 1.4 convolution_bitcast_fusion.2
  184.3 19.7 %all-reduce.8.cloned.1.call-done = f32[1,128,1152]{2,1,0:T(8,128)} async-done(((f32[1,128,1152]{2,1,0:T(8,128)}), f32[1,128,1152]{2,1,0:T(8,128)}) %all-reduce.8.cloned.1.call-update) | async-done | bytes 589840 | tf_op jit(solution)/shard_map/psum | solution.py:109
  203.9 2.5 fusion.13
  206.4 13.5 %all_gather.35 = f32[4,16,128]{2,1,0:T(8,128)S(1)} all-gather(f32[1,16,128]{2,1,0:T(8,128)S(1)} %fusion.13), channel_id=1, replica_groups=mesh['parts'=2,'step'=4,'frame'=2,'head'=2] {'step'}, dimensions={0}, use_global_device_ids=true | all-gather | bytes 40960 | tf_op jit(solution)/shard_map/all_gather | solution.py:14
  220.4 4.0 %fusion.6 = bf16[1,128,3,576]{1,3,2,0:T(8,128)(2,1)S(1)} fusion(bf16[1152,3,576]{2,0,1:T(8,128)(2,1)} %all-gather.3.cloned.1.call-done, f32[128,1152]{1,0:T(8,128)S(1)} %get-tuple-element.440, f32[128]{0:T(128)S(1)} %add_rsqrt_fusion.1, f32[1152]{0:T(1024)S(1)} %copy-done.6), kind=kOutput, calls=%fused_computation.26 | convolution fusion | flops 510271488 | bytes 5018624 | tf_op jit(solution)/shard_map/brd,dkq->brkq/dot_general | solution.py:76
  224.5 7.4 %all_gather.36 = bf16[1,256,2,576]{1,3,2,0:T(8,128)(2,1)S(1)} all-gather(bf16[1,128,2,576]{1,3,2,0:T(8,128)(2,1)S(1)} %slice.72), channel_id=1, replica_groups=mesh['parts'=2,'step'=4,'frame'=2,'head'=2] {'frame'}, dimensions={1}, use_global_device_ids=true | all-gather | bytes 884736 | tf_op jit(solution)/shard_map/all_gather | solution.py:82
  233.2 1.4 convolution_bitcast_fusion.1
  234.9 19.5 %all-reduce.10.cloned.1.call-done = f32[1,128,1152]{2,1,0:T(8,128)} async-done(((f32[1,128,1152]{2,1,0:T(8,128)}), f32[1,128,1152]{2,1,0:T(8,128)}) %all-reduce.10.cloned.1.call-update) | async-done | bytes 589840 | tf_op jit(solution)/shard_map/psum | solution.py:109
  254.4 2.5 fusion.11
  256.9 13.5 %all_gather.37 = f32[4,16,128]{2,1,0:T(8,128)S(1)} all-gather(f32[1,16,128]{2,1,0:T(8,128)S(1)} %fusion.11), channel_id=1, replica_groups=mesh['parts'=2,'step'=4,'frame'=2,'head'=2] {'step'}, dimensions={0}, use_global_device_ids=true | all-gather | bytes 40960 | tf_op jit(solution)/shard_map/all_gather | solution.py:14
  270.9 4.0 %fusion.7 = bf16[1,128,3,576]{1,3,2,0:T(8,128)(2,1)S(1)} fusion(bf16[1152,3,576]{2,0,1:T(8,128)(2,1)} %all-gather.3.cloned.1.call-done, f32[128,1152]{1,0:T(8,128)S(1)} %get-tuple-element.444, f32[128]{0:T(128)S(1)} %add_rsqrt_fusion, f32[1152]{0:T(1024)S(1)} %copy-done.6), kind=kOutput, calls=%fused_computation.27 | convolution fusion | flops 510271488 | bytes 5018624 | tf_op jit(solution)/shard_map/brd,dkq->brkq/dot_general | solution.py:76
  275.0 7.4 %all_gather.38 = bf16[1,256,2,576]{1,3,2,0:T(8,128)(2,1)S(1)} all-gather(bf16[1,128,2,576]{1,3,2,0:T(8,128)(2,1)S(1)} %slice.76), channel_id=1, replica_groups=mesh['parts'=2,'step'=4,'frame'=2,'head'=2] {'frame'}, dimensions={1}, use_global_device_ids=true | all-gather | bytes 884736 | tf_op jit(solution)/shard_map/all_gather | solution.py:82
  283.7 1.4 convolution_bitcast_fusion
  285.1 19.7 %all-reduce.12.cloned.1.call-done = f32[1,128,1152]{2,1,0:T(8,128)} async-done(((f32[1,128,1152]{2,1,0:T(8,128)}), f32[1,128,1152]{2,1,0:T(8,128)}) %all-reduce.12.cloned.1.call-update) | async-done | bytes 589840 | tf_op jit(solution)/shard_map/psum | solution.py:109
  304.9 2.5 fusion.9
  307.3 13.5 %all_gather.39 = f32[4,16,128]{2,1,0:T(8,128)S(1)} all-gather(f32[1,16,128]{2,1,0:T(8,128)S(1)} %fusion.9), channel_id=1, replica_groups=mesh['parts'=2,'step'=4,'frame'=2,'head'=2] {'step'}, dimensions={0}, use_global_device_ids=true | all-gather | bytes 40960 | tf_op jit(solution)/shard_map/all_gather | solution.py:14
  321.0 1.3 fusion.73
  322.2 22.0 %all-reduce = (f32[]{:T(128)}, f32[]{:T(128)}, f32[]{:T(128)}, f32[]{:T(128)}) all-reduce(f32[]{:T(128)} %get-tuple-element.383, f32[]{:T(128)} %get-tuple-element.384, f32[]{:T(128)} %get-tuple-element.385, f32[]{:T(128)} %get-tuple-element.382), channel_id=1, replica_groups=mesh['parts'=2,'step'=4,'frame'=2,'head'=2] {'step','frame'}, use_global_device_ids=true, to_apply=%region_33.34 | all-reduce | flops 4 | bytes 32 | tf_op jit(solution)/shard_map/psum | solution.py:120
  347.0 0.6 pad_maximum_fusion
  (92 shorter events, 8.4 us)
Async XLA Ops:
  7.2 2.2 copy-start
  7.2 2.4 copy-start.5
  7.2 2.4 copy-start.2
  7.2 2.4 copy-start.3
  7.2 89.7 %copy-start.6 = (f32[1152]{0:T(1024)S(1)}, f32[1152]{0:T(1024)}, u32[]{:S(2)}) copy-start(f32[1152]{0:T(1024)} %param.28) | copy-start | bytes 13828
  7.2 89.7 %all-gather.3.cloned.1.call-start = ((), (), s32[]{:S(2)}) async-start(), calls=%async_computation | async-start | bytes 5529600 | tf_op jit(solution)/shard_map/all_gather | solution.py:44
  8.0 124.3 %all-gather.5.cloned.1.call-start = ((), (), s32[]{:S(2)}) async-start(), calls=%async_computation.1 | async-start | bytes 1843200 | tf_op jit(solution)/shard_map/all_gather | solution.py:45
  8.7 144.2 %all-reduce.6.cloned.1.call-start = ((), (), s32[]{:S(2)}) async-start(), calls=%async_computation.2 | async-start | bytes 1179648 | tf_op jit(solution)/shard_map/psum | solution.py:109
  111.6 24.2 %copy-start.7 = (f32[128]{0:T(128)S(1)}, f32[128]{0:T(128)}, u32[]{:S(2)}) copy-start(f32[128]{0:T(128)} %param.25) | copy-start | bytes 1540
  111.6 24.2 %copy-start.8 = (f32[128]{0:T(128)S(1)}, f32[128]{0:T(128)}, u32[]{:S(2)}) copy-start(f32[128]{0:T(128)} %param.26) | copy-start | bytes 1540
  111.6 41.3 %copy-start.4 = (bf16[16,1152]{1,0:T(8,128)(2,1)S(1)}, bf16[16,1152]{1,0:T(8,128)(2,1)}, u32[]{:S(2)}) copy-start(bf16[16,1152]{1,0:T(8,128)(2,1)} %param.31) | copy-start | bytes 110596
  135.1 68.9 %all-reduce.8.cloned.1.call-start = ((), (), s32[]{:S(2)}) async-start(), calls=%async_computation.3 | async-start | bytes 1179648 | tf_op jit(solution)/shard_map/psum | solution.py:109
  181.4 1.4 copy-start.1
  184.2 70.2 %all-reduce.10.cloned.1.call-start = ((), (), s32[]{:S(2)}) async-start(), calls=%async_computation.4 | async-start | bytes 1179648 | tf_op jit(solution)/shard_map/psum | solution.py:109
  234.7 70.2 %all-reduce.12.cloned.1.call-start = ((), (), s32[]{:S(2)}) async-start(), calls=%async_computation.5 | async-start | bytes 1179648 | tf_op jit(solution)/shard_map/psum | solution.py:109
Sparse Core Ops, SparseCore 0:
  9.6 87.2 all-gather.2
  98.4 33.7 all-gather.4
  135.2 17.6 all-reduce.5
  184.3 19.5 all-reduce.7
  234.8 19.5 all-reduce.9
  285.2 19.5 all-reduce.11
where the time goes:
time: 355 us; the launch traced here: 354 us
  waiting for transfers between devices  184 us (52%)
  blocking collectives  108 us (30%)
  matrix products  38 us (11%)
  between operations  18.5 us (5%)
  other arithmetic  4.24 us (1%)
    all_gather x1, waiting for transfers between devices, local(): lax.all_gather(w_qkv, 'step', axis=0, tiled=True)  86.9 us
    psum x4, waiting for transfers between devices, local(): head_total = lax.psum(partial_value, 'head')  75.4 us
    all_gather x4, blocking collectives, entering(): everything = lax.all_gather(value, axis)  54.1 us
    all_gather x4, blocking collectives, local(): piece = lax.all_gather(keys_values, 'frame', axis=1, tiled=True)  31.6 us
    psum x1, blocking collectives, local(): summed = lax.psum(square_sum, ('step', 'frame'))  22 us
    all_gather x1, waiting for transfers between devices, local(): lax.all_gather(w_proj, 'step', axis=0, tiled=True)  20.7 us
    dot_general x4, matrix products, local(): jnp.einsum('brd,dkq->brkq', normed, w_qkv_all, preferred_element_type=jnp...  16.1 us
    dot_general x4, matrix products, local(): jnp.einsum('cd,brd->bcr', w_final, joined, preferred_element_type=jnp.flo...  9.96 us
  transfers between devices with their start and end apart: 6, of which 6 were waited for; matrix products, arithmetic and copies ran while one was open for 2% of the time, Pallas kernels for 0%

commit v1 on v0

--- a/solution.py
+++ b/solution.py
@@ -1,8 +1,11 @@
+import functools
 import math
 
 import jax
 import jax.numpy as jnp
 from jax import lax
+from jax.experimental import pallas as pl
+from jax.experimental.pallas import tpu as pltpu
 from jax.sharding import PartitionSpec as P
 
 HDIM = 72
@@ -26,7 +29,7 @@
     return first + second
 
 
-def local(
+def local_any(
     start_noise,
     position,
     time_table,
@@ -125,24 +128,412 @@
     return (trajectory, residual_norms)
 
 
+MESH = pl.DeviceIdType.MESH
+F32 = jnp.float32
+BF16 = jnp.bfloat16
+
+
+def dot(a, b, ca=1, cb=0):
+    return lax.dot_general(a, b, (((ca,), (cb,)), ((), ())), preferred_element_type=F32)
+
+
+def dot_exact(a, b):
+    return lax.dot_general(
+        a, b, (((1,), (0,)), ((), ())), precision=lax.Precision.HIGHEST, preferred_element_type=F32
+    )
+
+
+def two(a):
+    high = a.astype(BF16)
+    return high, (a - high.astype(F32)).astype(BF16)
+
+
+def evals_of(steps):
+    return [(i, j) for j in range(steps - 1) for i in range(min(j, ITERS - 1) + 1)] + [
+        (min(ITERS, steps) - 1, steps - 1)
+    ]
+
+
+def kernel(
+    S,
+    F,
+    H,
+    noise_ref,
+    pos_ref,
+    table_ref,
+    tidx_ref,
+    sidx_ref,
+    keep_ref,
+    coef_ref,
+    win_ref,
+    gain_ref,
+    wsend_ref,
+    msend_ref,
+    wfin_ref,
+    traj_ref,
+    res_ref,
+    w_buf,
+    m_buf,
+    pos_buf,
+    noise_buf,
+    meta_buf,
+    base_buf,
+    plane_buf,
+    line_buf,
+    ssem,
+    rsem,
+):
+    s, f, h = (lax.axis_index(a) for a in ("step", "frame", "head"))
+    PL = F * H
+    q_me = f * H + h
+    C, rows = noise_ref.shape
+    D = pos_ref.shape[1]
+    N = rows * F
+    pad = wsend_ref.shape[2]
+    lanes = table_ref.shape[0]
+
+    def step_peer(d):
+        return {"step": lax.rem(s + d, S)}
+
+    def plane_peer(d):
+        t = lax.rem(q_me + d, PL)
+        return {"frame": t // H, "head": lax.rem(t, H)}
+
+    def frame_peer(d):
+        return {"frame": lax.rem(f + d, F)}
+
+    barrier = pltpu.get_barrier_semaphore()
+    for d in range(1, S):
+        pl.semaphore_signal(barrier, inc=1, device_id=step_peer(d), device_id_type=MESH)
+    for d in range(1, PL):
+        pl.semaphore_signal(barrier, inc=1, device_id=plane_peer(d), device_id_type=MESH)
+
+    row_id = lax.broadcasted_iota(jnp.int32, (8, lanes), 0)
+    lane_id = lax.broadcasted_iota(jnp.int32, (1, lanes), 1)
+    hot_t = jnp.where(lane_id == tidx_ref[0], 1.0, 0.0)
+    hot_s = lane_id == sidx_ref[0]
+    keep = jnp.sum(jnp.where(hot_s, keep_ref[...], 0.0), axis=1, keepdims=True)
+    coef = jnp.sum(jnp.where(hot_s, coef_ref[...], 0.0), axis=1, keepdims=True)
+    meta_buf[s] = jnp.where(row_id == 0, hot_t, jnp.where(row_id == 1, keep, coef))
+    w_buf[s] = wsend_ref[s]
+    m_buf[s] = msend_ref[s]
+    pos_buf[f] = pos_ref[...]
+    noise_buf[f] = noise_ref[...]
+    pl.semaphore_wait(barrier, S - 1 + PL - 1)
+
+    count = [0]
+    started = []
+
+    def send(src, dst, peer):
+        k = count[0]
+        count[0] += 1
+        copy = pltpu.make_async_remote_copy(
+            src_ref=src,
+            dst_ref=dst,
+            send_sem=ssem.at[k],
+            recv_sem=rsem.at[k],
+            device_id=peer,
+            device_id_type=MESH,
+        )
+        copy.start()
+        started.append(copy)
+        return copy
+
+    order = sorted(range(1, S), key=lambda d: abs(d - S / 2))
+    early = [send(meta_buf.at[s], meta_buf.at[s], step_peer(d)) for d in order]
+    early += [send(noise_ref, noise_buf.at[f], frame_peer(d)) for d in range(1, F)]
+    early += [send(pos_ref, pos_buf.at[f], frame_peer(d)) for d in range(1, F)]
+    late = [
+        send(wsend_ref.at[lax.rem(s + d, S)], w_buf.at[s], step_peer(d)) for d in order
+    ]
+    late += [
+        send(msend_ref.at[lax.rem(s + d, S)], m_buf.at[s], step_peer(d)) for d in order
+    ]
+    for copy in early:
+        copy.wait_recv()
+
+    pos = pos_buf[...].reshape(N, D)
+    start = jnp.concatenate([noise_buf[i] for i in range(F)], axis=1)
+    metas = [meta_buf[j] for j in range(S)]
+    hot = jnp.concatenate(
+        [m[0:1] for m in metas] + [jnp.zeros((8 - S, lanes), F32)], axis=0
+    ).astype(BF16)
+    keeps = [jnp.concatenate([m[1:2, :rows]] * F, axis=1) for m in metas]
+    coefs = [jnp.concatenate([m[2:3, :rows]] * F, axis=1) for m in metas]
+    temb = dot(hot, table_ref[...])
+    temb_b = temb.astype(BF16)
+    gain = gain_ref[...]
+    w_in = win_ref[...]
+    posf = pos.astype(F32)
+    p_hi, p_lo = two(posf * gain)
+    side = jnp.concatenate(
+        [w_in.astype(F32), temb, jnp.zeros((128 - C - 8, D), F32)], axis=0
+    )
+    q_hi, q_lo = two(side * gain)
+    left = jnp.concatenate([p_hi, p_lo, q_hi, q_lo], axis=0)
+    ends = jnp.concatenate([w_in, wfin_ref[...]], axis=0)
+    ends_pos = dot(ends, pos, 1, 1)
+    ends_t = dot(ends, temb_b, 1, 1)
+    ends_in = dot(ends, w_in, 1, 1)
+    sq_hi, sq_lo = two(posf * posf)
+    ones = jnp.ones((8, D), BF16)
+    norm_p = dot(ones, sq_hi, 1, 1) + dot(ones, sq_lo, 1, 1)
+    cross = dot(temb_b, pos, 1, 1)
+    norm_t = jnp.sum(temb * temb, axis=1, keepdims=True)
+    norms = [norm_p[0:1] + 2.0 * cross[j : j + 1] + norm_t[j : j + 1] for j in range(S)]
+
+    for copy in late:
+        copy.wait_recv()
+
+    wide = dot(left, w_buf[...].reshape(D, pad))
+    by_pos = jnp.transpose(wide[0:N] + wide[N : 2 * N])
+    by_side = jnp.transpose(wide[2 * N : 2 * N + 128] + wide[2 * N + 128 :])
+    mix = m_buf[0]
+    for j in range(1, S):
+        mix = mix + m_buf[j]
+    scale = 1.4426950408889634 / math.sqrt(HDIM)
+
+    def table_of(t):
+        return jnp.concatenate(
+            [
+                t[0:HDIM] * scale,
+                t[HDIM : 2 * HDIM],
+                dot_exact(mix, t[2 * HDIM : 3 * HDIM]),
+            ],
+            axis=0,
+        )
+
+    tab_pos, tab_side = table_of(by_pos), table_of(by_side)
+    big_hi, big_lo = two(jnp.concatenate([tab_side[:, 0:C], ends_in], axis=0))
+    for j in range(S):
+        base_buf[j] = jnp.concatenate(
+            [
+                tab_pos + tab_side[:, C + j : C + j + 1],
+                2.0 * (ends_pos[0:C] + ends_t[0:C, j : j + 1]),
+                ends_pos[C : 2 * C] + ends_t[C : 2 * C, j : j + 1],
+            ],
+            axis=0,
+        )
+    QK = 2 * HDIM
+
+    def partial(x, j):
+        xb = x.astype(BF16)
+        lin = dot(big_hi, xb) + dot(big_lo, xb) + base_buf[j]
+        square = jnp.sum(xb.astype(F32) * lin[QK + C : QK + 2 * C], axis=0, keepdims=True)
+        square = jnp.maximum(square + norms[j], 0.0)
+        r = lax.rsqrt(square * (1.0 / D) + 1e-06)
+        q = (lin[0:HDIM] * r).astype(BF16)
+        k = (lin[HDIM:QK] * r).astype(BF16)
+        v_hi, v_lo = two(lin[QK : QK + C] * r)
+        scores = dot(k, q, 0, 0)
+        e = jnp.exp2(scores - jnp.max(scores, axis=0, keepdims=True)).astype(BF16)
+        o = dot(jnp.concatenate([v_hi, v_lo, jnp.ones((C, N), BF16)], axis=0), e)
+        out = (o[0:C] + o[C : 2 * C]) / o[2 * C : 2 * C + 1]
+        return out, lin[QK + 2 * C : QK + 3 * C]
+
+    keys = evals_of(S)
+    state, local_eps, drift, flying = {}, {}, {}, {}
+
+    def launch(key):
+        i, j = key
+        n = keys.index(key)
+        x = start
+        for m in range(j if i else 0):
+            x = x + drift[(min(i - 1, m), m)]
+        state[key] = x
+        part, local_eps[key] = partial(x, j)
+        plane_buf[n, q_me] = part
+        slot = plane_buf.at[n, q_me]
+        flying[key] = [send(slot, slot, plane_peer(d)) for d in range(1, PL)]
+
+    def relay(key):
+        n = keys.index(key)
+        for copy in flying[key]:
+            copy.wait_recv()
+        total = plane_buf[n, 0]
+        for i in range(1, PL):
+            total = total + plane_buf[n, i]
+        line_buf[n, s] = total
+        slot = line_buf.at[n, s]
+        flying[key] = [send(slot, slot, step_peer(d)) for d in order]
+
+    def land(key):
+        n, j = keys.index(key), key[1]
+        for copy in flying[key]:
+            copy.wait_recv()
+        total = local_eps[key]
+        for i in range(S):
+            total = total + line_buf[n, i]
+        drift[key] = keeps[j] * state[key] + coefs[j] * total
+
+    for act, key in PLAN:
+        {"launch": launch, "relay": relay, "land": land}[act](key)
+
+    old = [start] * S
+    norms_out = []
+    for it in range(ITERS):
+        new, run = [], start
+        for j in range(S):
+            new.append(run)
+            if j < S - 1:
+                run = run + drift[(min(it, j), j)]
+        square = jnp.zeros((1, 1), F32)
+        for j in range(S):
+            change = new[j] - old[j]
+            square = square + jnp.sum(
+                jnp.sum(change * change, axis=0, keepdims=True), axis=1, keepdims=True
+            )
+        norms_out.append(jnp.sqrt(square / (S * C * N) + 1e-06))
+        old = new
+    lane = lax.broadcasted_iota(jnp.int32, res_ref.shape, 1)
+    res = jnp.zeros(res_ref.shape, F32)
+    for it in range(ITERS):
+        res = jnp.where(lane == it, norms_out[it], res)
+    res_ref[...] = res
+    mine = jnp.zeros((C, N), F32)
+    for j in range(S):
+        mine = jnp.where(s == j, old[j] + drift[(min(ITERS - 1, j), j)], mine)
+    half = mine[:, 0:rows]
+    for i in range(1, F):
+        half = jnp.where(f == i, mine[:, i * rows : (i + 1) * rows], half)
+    traj_ref[0] = half
+    for copy in started:
+        copy.wait_send()
+
+
+PLAN = (
+    ("launch", (0, 0)),
+    ("launch", (0, 1)),
+    ("relay", (0, 0)),
+    ("launch", (0, 2)),
+    ("relay", (0, 1)),
+    ("land", (0, 0)),
+    ("launch", (1, 1)),
+    ("relay", (0, 2)),
+    ("relay", (1, 1)),
+    ("land", (0, 1)),
+    ("launch", (1, 2)),
+    ("land", (1, 1)),
+    ("launch", (2, 2)),
+    ("relay", (1, 2)),
+    ("relay", (2, 2)),
+    ("land", (0, 2)),
+    ("land", (1, 2)),
+    ("land", (2, 2)),
+    ("launch", (3, 3)),
+    ("relay", (3, 3)),
+    ("land", (3, 3)),
+)
+
+
+def local_heads(
+    start_noise,
+    position,
+    time_table,
+    time_index,
+    sched_index,
+    coef_keep,
+    coef_noise,
+    w_in,
+    norm_gain,
+    w_qkv,
+    w_proj,
+    w_final,
+):
+    S, F, H = (lax.axis_size(a) for a in ("step", "frame", "head"))
+    s, f = lax.axis_index("step"), lax.axis_index("frame")
+    R = w_qkv.shape[0]
+    C, rows = start_noise.shape
+    D = position.shape[1]
+    N = rows * F
+    PL = F * H
+    wq = w_qkv.reshape(R, 3, S, F, HDIM)
+    wq = lax.dynamic_index_in_dim(wq, f, axis=3, keepdims=False)
+    wq = jnp.transpose(wq, (2, 0, 1, 3)).reshape(S, R, 3 * HDIM)
+    pad = -(-3 * HDIM // 128) * 128
+    wq = jnp.pad(wq, ((0, 0), (0, 0), (0, pad - 3 * HDIM)))
+    wp = lax.dynamic_index_in_dim(w_proj.reshape(R, S, F, HDIM), f, axis=2, keepdims=False)
+    wf = lax.dynamic_slice_in_dim(w_final, s * R, R, axis=1)
+    mix = jnp.einsum("cr,rsk->sck", wf, wp, preferred_element_type=F32)
+    n_evals = len(evals_of(S))
+    n_sems = 3 * (S - 1) + 2 * (F - 1) + n_evals * (PL - 1 + S - 1)
+    vmem = pl.BlockSpec(memory_space=pltpu.VMEM)
+    smem = pl.BlockSpec(memory_space=pltpu.SMEM)
+    traj, res = pl.pallas_call(
+        functools.partial(kernel, S, F, H),
+        out_shape=(
+            jax.ShapeDtypeStruct((1, C, rows), F32),
+            jax.ShapeDtypeStruct((1, ITERS), F32),
+        ),
+        in_specs=[vmem, vmem, vmem, smem, smem] + [vmem] * 7,
+        out_specs=(vmem, vmem),
+        scratch_shapes=[
+            pltpu.VMEM((S, R, pad), BF16),
+            pltpu.VMEM((S, C, HDIM), F32),
+            pltpu.VMEM((F, rows, D), BF16),
+            pltpu.VMEM((F, C, rows), F32),
+            pltpu.VMEM((S, 8, time_table.shape[0]), F32),
+            pltpu.VMEM((S, 2 * HDIM + 3 * C, N), F32),
+            pltpu.VMEM((n_evals, PL, C, N), F32),
+            pltpu.VMEM((n_evals, S, C, N), F32),
+            pltpu.SemaphoreType.DMA((n_sems,)),
+            pltpu.SemaphoreType.DMA((n_sems,)),
+        ],
+        compiler_params=pltpu.CompilerParams(
+            collective_id=0, has_side_effects=True, vmem_limit_bytes=48 * 1024 * 1024
+        ),
+    )(
+        start_noise,
+        position,
+        time_table,
+        time_index,
+        sched_index,
+        coef_keep[None],
+        coef_noise[None],
+        w_in,
+        norm_gain[None],
+        wq,
+        mix,
+        w_final,
+    )
+    return traj, res.reshape(ITERS)
+
+
+def one_head_each(mesh, start_noise, time_index, w_qkv, time_table):
+    S, F, H = (mesh.shape[a] for a in ("step", "frame", "head"))
+    return (
+        S == ITERS
+        and time_index.shape[0] == S
+        and w_qkv.shape[2] == S * F * H * HDIM
+        and w_qkv.shape[0] % (16 * S) == 0
+        and start_noise.shape[1] % (128 * F) == 0
+        and start_noise.shape[1] // F <= time_table.shape[0]
+        and time_table.shape[0] % 128 == 0
+    )
+
+
 def solution(mesh):
-    return jax.shard_map(
-        local,
-        mesh=mesh,
-        in_specs=(
-            P("parts", "frame"),
-            P("frame", None),
-            P(),
-            P("step"),
-            P("step"),
-            P(),
-            P(),
-            P(),
-            P(),
-            P("step", None, "head"),
-            P("step", "head"),
-            P(),
-        ),
-        out_specs=(P("step", "parts", "frame"), P("parts")),
-        check_vma=False,
-    )
+    def call(*args):
+        fits = one_head_each(mesh, args[0], args[3], args[9], args[2])
+        return jax.shard_map(
+            local_heads if fits else local_any,
+            mesh=mesh,
+            in_specs=(
+                P("parts", "frame"),
+                P("frame", None),
+                P(),
+                P("step"),
+                P("step"),
+                P(),
+                P(),
+                P(),
+                P(),
+                P("step", None, "head"),
+                P("step", "head"),
+                P(),
+            ),
+            out_specs=(P("step", "parts", "frame"), P("parts")),
+            check_vma=False,
+        )(*args)
+
+    return call

time: 355 us -> 60.7 us (0.17)
  waiting for transfers between devices: 184 us -> 0 us
  blocking collectives: 108 us -> 0 us
  Pallas kernels: 0 us -> 53 us
  matrix products: 38 us -> 0.22 us
  between operations: 18.5 us -> 2.08 us
  other arithmetic: 4.24 us -> 0 us
  local copies, waits for them, and re-layouts: 0.92 us -> 5.13 us
    all_gather x2 -> x0, waiting for transfers between devices: 108 us -> none  [the longest x1 86.9 us: local(): lax.all_gather(w_qkv, 'step', axis=0, tiled=True)]
    all_gather x8 -> x0, blocking collectives: 85.7 us -> none  [the longest x4 54.1 us: entering(): everything = lax.all_gather(value, axis)]
    psum x4 -> x0, waiting for transfers between devices: 75.4 us -> none  [local(): head_total = lax.psum(partial_value, 'head')]
    pallas_call x0 -> x1, Pallas kernels: none -> 53 us  [local_heads(): pl.pallas_call(functools.partial(kernel, S, F, H), out_shape=(jax.ShapeDt...]
    dot_general x25 -> x1, matrix products: 38 us -> 0.22 us  [local_heads(): mix = jnp.einsum('cr,rsk->sck', wf, wp, preferred_element_type=F32)]
    psum x1 -> x0, blocking collectives: 22 us -> none  [local(): summed = lax.psum(square_sum, ('step', 'frame'))]
  transfers between devices with their start and end apart: 6 -> 0, of which waited for: 6 -> 0; matrix products, arithmetic and copies ran while one was open for 2% -> 0% of each run, Pallas kernels for 0% -> 0%
where the time goes in v1:
time: 60.7 us; the launch traced here: 60.4 us
  Pallas kernels  53 us (87%)
  local copies, waits for them, and re-layouts  5.13 us (8%)
  between operations  2.08 us (3%)
    pallas_call x1, Pallas kernels, local_heads(): pl.pallas_call(functools.partial(kernel, S, F, H), out_shape=(jax.ShapeDt...  53 us
    unnamed x20, local copies, waits for them, and re-layouts  3.91 us

profile of v1, /device:TPU:0, one launch (start us, length us, event | category | flops | bytes accessed | tf_op | source)
XLA Modules:
  0.0 60.4 jit_solution(7381316014734721161)
XLA Ops:
  1.9 0.7 %broadcast_in_dim.11.gain_ref = f32[1,1152]{1,0:T(1,128)S(1)} reshape(f32[1152]{0:T(1024)} %param.20) | data formatting | bytes 9216 | tf_op jit(solution)/shard_map/broadcast_in_dim | solution.py:494
  2.6 2.0 %copy.19 = bf16[288,3,576]{0,2,1:T(8,128)(2,1)S(1)} copy(bf16[288,3,576]{2,0,1:T(8,128)(2,1)} %param.21) | data formatting | bytes 1990656 | tf_op args[9]
  4.6 0.1 dynamic-slice_bitcast_fusion
  4.7 0.1 copy.20
  4.8 0.0 copy-start.7
  4.8 0.0 copy-start.2
  4.8 0.3 copy.21
  5.1 0.0 copy-start
  5.1 0.0 copy-start.1
  5.1 0.0 copy-start.3
  5.1 0.0 copy-start.4
  5.1 0.0 copy-start.5
  5.1 0.0 copy-start.6
  5.2 0.1 pad.4.wsend_ref
  5.3 0.5 copy-done.7
  5.8 0.2 copy.22
  6.0 0.0 copy-done.2
  6.0 0.2 convolution_bitcast_fusion.msend_ref
  6.2 0.0 copy-done
  6.2 0.0 copy-done.1
  6.2 0.0 copy-done.3
  6.3 0.0 copy-done.4
  6.3 0.0 copy-done.5
  6.3 0.0 copy-done.6
  6.3 53.0 %shard_map.131 = (f32[1,16,128]{2,1,0:T(8,128)S(1)}, f32[1,4]{1,0:T(1,128)S(1)}) custom-call(f32[16,128]{1,0:T(8,128)S(1)} %copy-done.4, bf16[128,1152]{1,0:T(8,128)(2,1)S(1)} %copy-done, bf16[128,1152]{1,0:T(8,128)(2,1)S(1)} %copy-done.1, s32[1]{0:T(128)S(6)} %copy.25.tidx_ref, s32[1]{0:T(128)S(6)} %copy.26.sidx_ref, f32[1,128]{1,0:T(1,128)S(1)} %bitcast.18, ...), custom_call_target="tpu_custom_call" | custom-call | tf_op jit(solution)/shard_map/pallas_call | solution.py:462
  59.3 0.6 copy.27
  59.9 0.5 copy.28
Async XLA Ops:
  4.8 1.0 %copy-start.7 = (bf16[288,576]{1,0:T(8,128)(2,1)S(1)}, bf16[288,576]{1,0:T(8,128)(2,1)}, u32[]{:S(2)}) copy-start(bf16[288,576]{1,0:T(8,128)(2,1)} %param.22) | copy-start | bytes 995332
  4.8 1.2 %copy-start.2 = (bf16[16,1152]{1,0:T(8,128)(2,1)S(1)}, bf16[16,1152]{1,0:T(8,128)(2,1)}, u32[]{:S(2)}) copy-start(bf16[16,1152]{1,0:T(8,128)(2,1)} %wfin_ref.1) | copy-start | bytes 110596
  5.1 1.2 %copy-start = (bf16[128,1152]{1,0:T(8,128)(2,1)S(1)}, bf16[128,1152]{1,0:T(8,128)(2,1)}, u32[]{:S(2)}) copy-start(bf16[128,1152]{1,0:T(8,128)(2,1)} %pos_ref.1) | copy-start | bytes 884740
  5.1 1.2 %copy-start.1 = (bf16[128,1152]{1,0:T(8,128)(2,1)S(1)}, bf16[128,1152]{1,0:T(8,128)(2,1)}, u32[]{:S(2)}) copy-start(bf16[128,1152]{1,0:T(8,128)(2,1)} %table_ref.1) | copy-start | bytes 884740
  5.1 1.2 %copy-start.3 = (bf16[16,1152]{1,0:T(8,128)(2,1)S(1)}, bf16[16,1152]{1,0:T(8,128)(2,1)}, u32[]{:S(2)}) copy-start(bf16[16,1152]{1,0:T(8,128)(2,1)} %win_ref.1) | copy-start | bytes 110596
  5.1 1.2 %copy-start.4 = (f32[16,128]{1,0:T(8,128)S(1)}, f32[16,128]{1,0:T(8,128)}, u32[]{:S(2)}) copy-start(f32[16,128]{1,0:T(8,128)} %noise_ref.1) | copy-start | bytes 24580
  5.1 1.2 %copy-start.5 = (f32[128]{0:T(128)S(1)}, f32[128]{0:T(128)}, u32[]{:S(2)}) copy-start(f32[128]{0:T(128)} %param.17) | copy-start | bytes 1540
  5.1 1.2 %copy-start.6 = (f32[128]{0:T(128)S(1)}, f32[128]{0:T(128)}, u32[]{:S(2)}) copy-start(f32[128]{0:T(128)} %param.18) | copy-start | bytes 1540

commit v2 on v1

--- a/solution.py
+++ b/solution.py
@@ -158,20 +158,28 @@
     S,
     F,
     H,
-    noise_ref,
-    pos_ref,
-    table_ref,
+    noise_hbm,
+    pos_hbm,
+    table_hbm,
     tidx_ref,
     sidx_ref,
+    keep_hbm,
+    coef_hbm,
+    win_hbm,
+    gain_hbm,
+    wqkv_hbm,
+    wproj_hbm,
+    wfin_hbm,
+    traj_ref,
+    res_ref,
+    table_ref,
     keep_ref,
     coef_ref,
     win_ref,
     gain_ref,
-    wsend_ref,
-    msend_ref,
+    wqkv_ref,
+    wproj_ref,
     wfin_ref,
-    traj_ref,
-    res_ref,
     w_buf,
     m_buf,
     pos_buf,
@@ -180,16 +188,37 @@
     base_buf,
     plane_buf,
     line_buf,
+    wsend_ref,
+    msend_ref,
     ssem,
     rsem,
 ):
     s, f, h = (lax.axis_index(a) for a in ("step", "frame", "head"))
+    loads = [
+        pltpu.make_async_copy(src, dst, ssem.at[ssem.shape[0] - 1 - n])
+        for n, (src, dst) in enumerate(
+            (
+                (pos_hbm, pos_buf.at[f]),
+                (noise_hbm, noise_buf.at[f]),
+                (keep_hbm, keep_ref),
+                (coef_hbm, coef_ref),
+                (wqkv_hbm, wqkv_ref),
+                (wproj_hbm, wproj_ref),
+                (wfin_hbm, wfin_ref),
+                (table_hbm, table_ref),
+                (win_hbm, win_ref),
+                (gain_hbm, gain_ref),
+            )
+        )
+    ]
+    for copy in loads:
+        copy.start()
     PL = F * H
     q_me = f * H + h
-    C, rows = noise_ref.shape
-    D = pos_ref.shape[1]
+    C, rows = noise_buf.shape[1:]
+    D = pos_buf.shape[2]
     N = rows * F
-    pad = wsend_ref.shape[2]
+    pad = w_buf.shape[2]
     lanes = table_ref.shape[0]
 
     def step_peer(d):
@@ -208,6 +237,8 @@
     for d in range(1, PL):
         pl.semaphore_signal(barrier, inc=1, device_id=plane_peer(d), device_id_type=MESH)
 
+    for copy in loads[:4]:
+        copy.wait()
     row_id = lax.broadcasted_iota(jnp.int32, (8, lanes), 0)
     lane_id = lax.broadcasted_iota(jnp.int32, (1, lanes), 1)
     hot_t = jnp.where(lane_id == tidx_ref[0], 1.0, 0.0)
@@ -215,10 +246,6 @@
     keep = jnp.sum(jnp.where(hot_s, keep_ref[...], 0.0), axis=1, keepdims=True)
     coef = jnp.sum(jnp.where(hot_s, coef_ref[...], 0.0), axis=1, keepdims=True)
     meta_buf[s] = jnp.where(row_id == 0, hot_t, jnp.where(row_id == 1, keep, coef))
-    w_buf[s] = wsend_ref[s]
-    m_buf[s] = msend_ref[s]
-    pos_buf[f] = pos_ref[...]
-    noise_buf[f] = noise_ref[...]
     pl.semaphore_wait(barrier, S - 1 + PL - 1)
 
     count = [0]
@@ -241,14 +268,41 @@
 
     order = sorted(range(1, S), key=lambda d: abs(d - S / 2))
     early = [send(meta_buf.at[s], meta_buf.at[s], step_peer(d)) for d in order]
-    early += [send(noise_ref, noise_buf.at[f], frame_peer(d)) for d in range(1, F)]
-    early += [send(pos_ref, pos_buf.at[f], frame_peer(d)) for d in range(1, F)]
+    early += [send(noise_buf.at[f], noise_buf.at[f], frame_peer(d)) for d in range(1, F)]
+    early += [send(pos_buf.at[f], pos_buf.at[f], frame_peer(d)) for d in range(1, F)]
+    for copy in loads[4:7]:
+        copy.wait()
+    R = wqkv_ref.shape[1]
+    for i in range(F):
+
+        @pl.when(f == i)
+        def _():
+            for t in range(S):
+                low = (t * F + i) * HDIM
+                parts = [wqkv_ref[p, :, low : low + HDIM] for p in range(3)]
+                parts.append(jnp.zeros((R, pad - 3 * HDIM), BF16))
+                wsend_ref[t] = jnp.concatenate(parts, axis=1)
+
     late = [
         send(wsend_ref.at[lax.rem(s + d, S)], w_buf.at[s], step_peer(d)) for d in order
     ]
+    rows_of = wfin_ref[:, 0:R].astype(F32)
+    for j in range(1, S):
+        rows_of = jnp.where(s == j, wfin_ref[:, j * R : (j + 1) * R].astype(F32), rows_of)
+    folded = dot(rows_of.astype(BF16), wproj_ref[...])
+    for t in range(S):
+        picked = folded[:, t * F * HDIM : (t * F + 1) * HDIM]
+        for i in range(1, F):
+            low = (t * F + i) * HDIM
+            picked = jnp.where(f == i, folded[:, low : low + HDIM], picked)
+        msend_ref[t] = picked
     late += [
         send(msend_ref.at[lax.rem(s + d, S)], m_buf.at[s], step_peer(d)) for d in order
     ]
+    w_buf[s] = wsend_ref[s]
+    m_buf[s] = msend_ref[s]
+    for copy in loads[7:]:
+        copy.wait()
     for copy in early:
         copy.wait_recv()
 
@@ -342,7 +396,7 @@
             x = x + drift[(min(i - 1, m), m)]
         state[key] = x
         part, local_eps[key] = partial(x, j)
-        plane_buf[n, q_me] = part
+        plane_buf[n, q_me] = part.astype(BF16)
         slot = plane_buf.at[n, q_me]
         flying[key] = [send(slot, slot, plane_peer(d)) for d in range(1, PL)]
 
@@ -350,10 +404,10 @@
         n = keys.index(key)
         for copy in flying[key]:
             copy.wait_recv()
-        total = plane_buf[n, 0]
+        total = plane_buf[n, 0].astype(F32)
         for i in range(1, PL):
-            total = total + plane_buf[n, i]
-        line_buf[n, s] = total
+            total = total + plane_buf[n, i].astype(F32)
+        line_buf[n, s] = total.astype(BF16)
         slot = line_buf.at[n, s]
         flying[key] = [send(slot, slot, step_peer(d)) for d in order]
 
@@ -363,7 +417,7 @@
             copy.wait_recv()
         total = local_eps[key]
         for i in range(S):
-            total = total + line_buf[n, i]
+            total = total + line_buf[n, i].astype(F32)
         drift[key] = keeps[j] * state[key] + coefs[j] * total
 
     for act, key in PLAN:
@@ -441,46 +495,49 @@
     w_final,
 ):
     S, F, H = (lax.axis_size(a) for a in ("step", "frame", "head"))
-    s, f = lax.axis_index("step"), lax.axis_index("frame")
     R = w_qkv.shape[0]
     C, rows = start_noise.shape
     D = position.shape[1]
     N = rows * F
     PL = F * H
-    wq = w_qkv.reshape(R, 3, S, F, HDIM)
-    wq = lax.dynamic_index_in_dim(wq, f, axis=3, keepdims=False)
-    wq = jnp.transpose(wq, (2, 0, 1, 3)).reshape(S, R, 3 * HDIM)
     pad = -(-3 * HDIM // 128) * 128
-    wq = jnp.pad(wq, ((0, 0), (0, 0), (0, pad - 3 * HDIM)))
-    wp = lax.dynamic_index_in_dim(w_proj.reshape(R, S, F, HDIM), f, axis=2, keepdims=False)
-    wf = lax.dynamic_slice_in_dim(w_final, s * R, R, axis=1)
-    mix = jnp.einsum("cr,rsk->sck", wf, wp, preferred_element_type=F32)
     n_evals = len(evals_of(S))
     n_sems = 3 * (S - 1) + 2 * (F - 1) + n_evals * (PL - 1 + S - 1)
     vmem = pl.BlockSpec(memory_space=pltpu.VMEM)
     smem = pl.BlockSpec(memory_space=pltpu.SMEM)
+    here = pl.BlockSpec(memory_space=pl.ANY)
     traj, res = pl.pallas_call(
         functools.partial(kernel, S, F, H),
         out_shape=(
             jax.ShapeDtypeStruct((1, C, rows), F32),
             jax.ShapeDtypeStruct((1, ITERS), F32),
         ),
-        in_specs=[vmem, vmem, vmem, smem, smem] + [vmem] * 7,
+        in_specs=[here, here, here, smem, smem] + [here] * 7,
         out_specs=(vmem, vmem),
         scratch_shapes=[
+            pltpu.VMEM(time_table.shape, BF16),
+            pltpu.VMEM((1, coef_keep.shape[0]), F32),
+            pltpu.VMEM((1, coef_noise.shape[0]), F32),
+            pltpu.VMEM(w_in.shape, BF16),
+            pltpu.VMEM((1, D), F32),
+            pltpu.VMEM((3, R, w_qkv.shape[2]), BF16),
+            pltpu.VMEM(w_proj.shape, BF16),
+            pltpu.VMEM(w_final.shape, BF16),
             pltpu.VMEM((S, R, pad), BF16),
             pltpu.VMEM((S, C, HDIM), F32),
             pltpu.VMEM((F, rows, D), BF16),
             pltpu.VMEM((F, C, rows), F32),
             pltpu.VMEM((S, 8, time_table.shape[0]), F32),
             pltpu.VMEM((S, 2 * HDIM + 3 * C, N), F32),
-            pltpu.VMEM((n_evals, PL, C, N), F32),
-            pltpu.VMEM((n_evals, S, C, N), F32),
-            pltpu.SemaphoreType.DMA((n_sems,)),
+            pltpu.VMEM((n_evals, PL, C, N), BF16),
+            pltpu.VMEM((n_evals, S, C, N), BF16),
+            pltpu.VMEM((S, R, pad), BF16),
+            pltpu.VMEM((S, C, HDIM), F32),
+            pltpu.SemaphoreType.DMA((n_sems + 10,)),
             pltpu.SemaphoreType.DMA((n_sems,)),
         ],
         compiler_params=pltpu.CompilerParams(
-            collective_id=0, has_side_effects=True, vmem_limit_bytes=48 * 1024 * 1024
+            collective_id=0, has_side_effects=True, vmem_limit_bytes=60 * 1024 * 1024
         ),
     )(
         start_noise,
@@ -492,8 +549,8 @@
         coef_noise[None],
         w_in,
         norm_gain[None],
-        wq,
-        mix,
+        jnp.transpose(w_qkv, (1, 0, 2)),
+        w_proj,
         w_final,
     )
     return traj, res.reshape(ITERS)

time: 60.7 us -> 57.9 us (0.954)
  local copies, waits for them, and re-layouts: 5.13 us -> 3.73 us
  Pallas kernels: 53 us -> 51.9 us
    unnamed x20 -> x2, local copies, waits for them, and re-layouts: 3.91 us -> 2.43 us
    pallas_call x1, Pallas kernels: 53 us -> 51.9 us  [local_heads(): pl.pallas_call(functools.partial(kernel, S, F, H), out_shape=(jax.ShapeDt...]
where the time goes in v2:
time: 57.9 us; the launch traced here: 57.6 us
  Pallas kernels  51.9 us (90%)
  local copies, waits for them, and re-layouts  3.73 us (6%)
  between operations  1.93 us (3%)
    pallas_call x1, Pallas kernels, local_heads(): pl.pallas_call(functools.partial(kernel, S, F, H), out_shape=(jax.ShapeDt...  51.9 us
    unnamed x2, local copies, waits for them, and re-layouts  2.43 us
    broadcast_in_dim x1, local copies, waits for them, and re-layouts, local_heads(): norm_gain[None]  1.29 us

profile of v2, /device:TPU:0, one launch (start us, length us, event | category | flops | bytes accessed | tf_op | source)
XLA Modules:
  0.0 57.6 jit_solution(1970917979121021677)
XLA Ops:
  1.9 1.3 %broadcast_in_dim.11.gain_hbm = f32[1,1152]{1,0:T(1,128)} reshape(f32[1152]{0:T(1024)} %param.20) | data formatting | bytes 9216 | tf_op jit(solution)/shard_map/broadcast_in_dim | solution.py:551
  3.2 51.9 %shard_map.131 = (f32[1,16,128]{2,1,0:T(8,128)}, f32[1,4]{1,0:T(1,128)}) custom-call(f32[16,128]{1,0:T(8,128)} %noise_hbm.1, bf16[128,1152]{1,0:T(8,128)(2,1)} %pos_hbm.1, bf16[128,1152]{1,0:T(8,128)(2,1)} %table_hbm.1, s32[1]{0:T(128)S(6)} %copy.16.tidx_ref, s32[1]{0:T(128)S(6)} %copy.17.sidx_ref, f32[1,128]{1,0:T(1,128)} %bitcast.5, f32[1,128]{1,0:T(1,128)} %bitcast.6, ...), custom_call_target="tpu_custom_call" | custom-call | tf_op jit(solution)/shard_map/pallas_call | solution.py:509
  55.1 1.3 %copy.18 = f32[1,16,128]{2,1,0:T(8,128)} copy(f32[1,16,128]{2,1,0:T(8,128)} %get-tuple-element.8) | data formatting | bytes 16384
  56.4 1.1 %copy.19 = f32[4]{0:T(128)} copy(f32[4]{0:T(128)} %bitcast.7) | data formatting | bytes 32

commit v3 on v2

--- a/solution.py
+++ b/solution.py
@@ -231,7 +231,14 @@
     def frame_peer(d):
         return {"frame": lax.rem(f + d, F)}
 
+    Y, y = lax.axis_size("parts"), lax.axis_index("parts")
+
+    def part_peer(d):
+        return {"parts": lax.rem(y + d, Y)}
+
     barrier = pltpu.get_barrier_semaphore()
+    for d in range(1, Y):
+        pl.semaphore_signal(barrier, inc=1, device_id=part_peer(d), device_id_type=MESH)
     for d in range(1, S):
         pl.semaphore_signal(barrier, inc=1, device_id=step_peer(d), device_id_type=MESH)
     for d in range(1, PL):
@@ -246,7 +253,7 @@
     keep = jnp.sum(jnp.where(hot_s, keep_ref[...], 0.0), axis=1, keepdims=True)
     coef = jnp.sum(jnp.where(hot_s, coef_ref[...], 0.0), axis=1, keepdims=True)
     meta_buf[s] = jnp.where(row_id == 0, hot_t, jnp.where(row_id == 1, keep, coef))
-    pl.semaphore_wait(barrier, S - 1 + PL - 1)
+    pl.semaphore_wait(barrier, S - 1 + PL - 1 + Y - 1)
 
     count = [0]
     started = []
@@ -283,9 +290,12 @@
                 parts.append(jnp.zeros((R, pad - 3 * HDIM), BF16))
                 wsend_ref[t] = jnp.concatenate(parts, axis=1)
 
-    late = [
-        send(wsend_ref.at[lax.rem(s + d, S)], w_buf.at[s], step_peer(d)) for d in order
+    share = pl.ds(pl.multiple_of(y * (R // Y), 16), R // Y)
+    shares = [
+        send(wsend_ref.at[lax.rem(s + d, S), share], w_buf.at[s, share], step_peer(d))
+        for d in order
     ]
+    late = []
     rows_of = wfin_ref[:, 0:R].astype(F32)
     for j in range(1, S):
         rows_of = jnp.where(s == j, wfin_ref[:, j * R : (j + 1) * R].astype(F32), rows_of)
@@ -336,6 +346,10 @@
     norm_t = jnp.sum(temb * temb, axis=1, keepdims=True)
     norms = [norm_p[0:1] + 2.0 * cross[j : j + 1] + norm_t[j : j + 1] for j in range(S)]
 
+    for d, copy in zip(order, shares):
+        copy.wait_recv()
+        slot = w_buf.at[lax.rem(s + S - d, S), share]
+        late += [send(slot, slot, part_peer(e)) for e in range(1, Y)]
     for copy in late:
         copy.wait_recv()
 
@@ -502,7 +516,7 @@
     PL = F * H
     pad = -(-3 * HDIM // 128) * 128
     n_evals = len(evals_of(S))
-    n_sems = 3 * (S - 1) + 2 * (F - 1) + n_evals * (PL - 1 + S - 1)
+    n_sems = (2 + lax.axis_size("parts")) * (S - 1) + 2 * (F - 1) + n_evals * (PL - 1 + S - 1)
     vmem = pl.BlockSpec(memory_space=pltpu.VMEM)
     smem = pl.BlockSpec(memory_space=pltpu.SMEM)
     here = pl.BlockSpec(memory_space=pl.ANY)
@@ -562,7 +576,7 @@
         S == ITERS
         and time_index.shape[0] == S
         and w_qkv.shape[2] == S * F * H * HDIM
-        and w_qkv.shape[0] % (16 * S) == 0
+        and w_qkv.shape[0] % (16 * S * mesh.shape["parts"]) == 0
         and start_noise.shape[1] % (128 * F) == 0
         and start_noise.shape[1] // F <= time_table.shape[0]
         and time_table.shape[0] % 128 == 0

time: 57.9 us -> 58.1 us (level)
  no operation moved by 1% of the time
where the time goes in v3:
time: 58.1 us; the launch traced here: 57.8 us
  Pallas kernels  52.1 us (90%)
  local copies, waits for them, and re-layouts  3.73 us (6%)
  between operations  1.93 us (3%)
    pallas_call x1, Pallas kernels, local_heads(): pl.pallas_call(functools.partial(kernel, S, F, H), out_shape=(jax.ShapeDt...  52.1 us
    unnamed x2, local copies, waits for them, and re-layouts  2.43 us
    broadcast_in_dim x1, local copies, waits for them, and re-layouts, local_heads(): norm_gain[None]  1.29 us

profile of v3, /device:TPU:0, one launch (start us, length us, event | category | flops | bytes accessed | tf_op | source)
XLA Modules:
  0.0 57.8 jit_solution(9130811170115529404)
XLA Ops:
  1.9 1.3 %broadcast_in_dim.11.gain_hbm = f32[1,1152]{1,0:T(1,128)} reshape(f32[1152]{0:T(1024)} %param.20) | data formatting | bytes 9216 | tf_op jit(solution)/shard_map/broadcast_in_dim | solution.py:565
  3.2 52.1 %shard_map.131 = (f32[1,16,128]{2,1,0:T(8,128)}, f32[1,4]{1,0:T(1,128)}) custom-call(f32[16,128]{1,0:T(8,128)} %noise_hbm.1, bf16[128,1152]{1,0:T(8,128)(2,1)} %pos_hbm.1, bf16[128,1152]{1,0:T(8,128)(2,1)} %table_hbm.1, s32[1]{0:T(128)S(6)} %copy.16.tidx_ref, s32[1]{0:T(128)S(6)} %copy.17.sidx_ref, f32[1,128]{1,0:T(1,128)} %bitcast.5, f32[1,128]{1,0:T(1,128)} %bitcast.6, ...), custom_call_target="tpu_custom_call" | custom-call | tf_op jit(solution)/shard_map/pallas_call | solution.py:523
  55.3 1.3 %copy.18 = f32[1,16,128]{2,1,0:T(8,128)} copy(f32[1,16,128]{2,1,0:T(8,128)} %get-tuple-element.8) | data formatting | bytes 16384
  56.6 1.1 %copy.19 = f32[4]{0:T(128)} copy(f32[4]{0:T(128)} %bitcast.7) | data formatting | bytes 32
